TPU v7x, 128 devices: a whole 4x4x4 slice. The times are simulated.
128 devices in a mesh: group: 8 (over z, core), tensor: 16 (over y, x).
Axes of the slice: x: 4, y: 4, z: 4, core: 2. Of those that a mesh axis runs over, the one named last changes fastest.
Arguments:
- hidden_rows: bfloat16 [3072, 8192], P('group', 'tensor'), may hold values from -6 to 6
- attn_rows: bfloat16 [3072, 8192], P('group', 'tensor'), may hold values from -6 to 6
- q_weight: bfloat16 [8192, 8192], P(None, 'tensor'), may hold values from -0.0625 to 0.0625
- o_weight: bfloat16 [8192, 8192], P('tensor'), may hold values from -0.0625 to 0.0625
- owner_table: int32 [64], replicated, may hold values from 0 to 63, as said below
- group_adapters: int32 [8, 8], replicated, may hold values from 0 to 63, as said below
- req_slot: int32 [8, 16], P('group'), may hold values from 0 to 7
- req_len: int32 [8, 16], P('group'), may hold values from 1 to 96, 384 in all within a row
- qa_store: bfloat16 [64, 8192, 64], P('group', 'tensor'), may hold values from -0.0625 to 0.0625
- qb_store: bfloat16 [64, 64, 8192], P('group', None, 'tensor'), may hold values from -0.75 to 0.75
- oa_store: bfloat16 [64, 8192, 64], P('group', 'tensor'), may hold values from -0.0625 to 0.0625
- ob_store: bfloat16 [64, 64, 8192], P('group', None, 'tensor'), may hold values from -0.75 to 0.75
Outputs:
- queries: bfloat16 [3072, 8192], P('group', 'tensor')
- attn_out: bfloat16 [3072, 8192], P('group')
Inputs may be any that keep to these rules, and one draw needn't show every extreme that they name: A permutation: adapter a sits at storage index owner_table[a], held by index owner_table[a] // 8 of group. `group_adapters`: each row names 8 distinct adapters, exactly 1 of them held by each index of group; different groups may name the same adapter.
All inputs are finite; a program needn't handle non-finite values.
Results may differ from a plain program's by a relative error of at most 0.001.
Values may be sent and summed in bfloat16 or wider, within the bound.
A program may use at most 128 MiB of HBM per device.

v0:
```python
import jax
import jax.numpy as jnp
from jax import lax
from jax.sharding import PartitionSpec as P

ADAPTER_SCALE = 0.5


def slot_onehot(lengths, slot_ids, row_count, slot_count):
    req_ends = jnp.cumsum(lengths)
    req_starts = req_ends - lengths
    position = jnp.arange(row_count, dtype=jnp.int32)[:, None]
    inside = ((position >= req_starts[None, :]) & (position < req_ends[None, :])).astype(jnp.int32)
    slot_row = jnp.sum(inside * slot_ids[None, :], axis=1)
    return slot_row[:, None] == jnp.arange(slot_count, dtype=jnp.int32)[None, :]


def down_select(rows_in, down_all, onehot):
    slot_count, width_part, rank_size = down_all.shape
    down_flat = jnp.transpose(down_all, (1, 0, 2)).reshape(width_part, slot_count * rank_size)
    partial_down = jnp.dot(rows_in, down_flat, preferred_element_type=jnp.float32)
    partial_down = partial_down.reshape(rows_in.shape[0], slot_count, rank_size)
    return jnp.sum(onehot.astype(jnp.float32)[:, :, None] * partial_down, axis=1)


def up_product(down_rows, up_all, onehot):
    slot_count, rank_size, width_part = up_all.shape
    expanded_rows = onehot.astype(jnp.float32)[:, :, None] * down_rows[:, None, :]
    expanded_rows = expanded_rows.reshape(down_rows.shape[0], slot_count * rank_size)
    up_weight_flat = up_all.reshape(slot_count * rank_size, width_part).astype(jnp.float32)
    return ADAPTER_SCALE * jnp.dot(
        expanded_rows,
        up_weight_flat,
        precision=lax.Precision.HIGHEST,
        preferred_element_type=jnp.float32,
    )


def body(
    hidden_rows,
    attn_rows,
    q_weight,
    o_weight,
    owner_table,
    group_adapters,
    req_slot,
    req_len,
    qa_store,
    qb_store,
    oa_store,
    ob_store,
):
    slot_count = group_adapters.shape[1]
    groups = lax.axis_size("group")
    own_group = lax.axis_index("group")
    held_count = qa_store.shape[0]
    storage = jnp.take(owner_table, group_adapters, axis=0)
    per_owner = slot_count // groups
    owners = storage // held_count
    local_idx = storage % held_count
    same_owner = owners[:, :, None] == owners[:, None, :]
    slot_iota = jnp.arange(slot_count, dtype=jnp.int32)
    earlier = slot_iota[None, :] < slot_iota[:, None]
    order_rank = jnp.sum((same_owner & earlier[None, :, :]).astype(jnp.int32), axis=2)
    chosen = (owners[:, None, :] == own_group) & (
        order_rank[:, None, :] == jnp.arange(per_owner, dtype=jnp.int32)[None, :, None]
    )
    send_index = jnp.sum(chosen.astype(jnp.int32) * local_idx[:, None, :], axis=2).reshape(-1)
    filled = jnp.any(chosen, axis=2).reshape(-1)

    def pack(stored):
        gathered = jnp.take(stored, send_index, axis=0)
        return gathered * filled[:, None, None].astype(stored.dtype)

    received = (
        lax.all_to_all(pack(qa_store), "group", split_axis=0, concat_axis=0, tiled=True),
        lax.all_to_all(pack(qb_store), "group", split_axis=0, concat_axis=0, tiled=True),
        lax.all_to_all(pack(oa_store), "group", split_axis=0, concat_axis=0, tiled=True),
        lax.all_to_all(pack(ob_store), "group", split_axis=0, concat_axis=0, tiled=True),
    )
    owners_mine = lax.dynamic_index_in_dim(owners, own_group, 0, keepdims=False)
    rank_mine = lax.dynamic_index_in_dim(order_rank, own_group, 0, keepdims=False)
    slot_index = owners_mine * per_owner + rank_mine
    qa_used = jnp.take(received[0], slot_index, axis=0)
    qb_used = jnp.take(received[1], slot_index, axis=0)
    output_down_picked = jnp.take(received[2], slot_index, axis=0)
    ob_used = jnp.take(received[3], slot_index, axis=0)
    row_count = hidden_rows.shape[0]
    onehot = slot_onehot(req_len[0], req_slot[0], row_count, slot_count)
    q_partial = down_select(hidden_rows, qa_used, onehot)
    output_partial_sum = down_select(attn_rows, output_down_picked, onehot)
    q_down, o_down = lax.psum((q_partial, output_partial_sum), "tensor")
    base_query = jnp.dot(
        lax.all_gather(hidden_rows, "tensor", axis=1, tiled=True),
        q_weight,
        preferred_element_type=jnp.float32,
    )
    queries = (base_query + up_product(q_down, qb_used, onehot)).astype(jnp.bfloat16)
    o_term = jnp.dot(attn_rows, o_weight, preferred_element_type=jnp.float32)
    o_up = up_product(o_down, ob_used, onehot)
    width_part = o_up.shape[1]
    column = lax.axis_index("tensor") * width_part
    current = lax.dynamic_slice_in_dim(o_term, column, width_part, 1)
    o_term = lax.dynamic_update_slice_in_dim(o_term, current + o_up, column, 1)
    attn_out = lax.psum(o_term, "tensor").astype(jnp.bfloat16)
    return (queries, attn_out)


def solution(mesh):
    return jax.shard_map(
        body,
        mesh=mesh,
        in_specs=(
            P("group", "tensor"),
            P("group", "tensor"),
            P(None, "tensor"),
            P("tensor", None),
            P(),
            P(),
            P("group", None),
            P("group", None),
            P("group", "tensor", None),
            P("group", None, "tensor"),
            P("group", "tensor", None),
            P("group", None, "tensor"),
        ),
        out_specs=(P("group", "tensor"), P("group", None)),
        check_vma=False,
    )
```

profile of v0, /device:TPU:1, one launch (start us, length us, event | category | flops | bytes accessed | tf_op | source)
XLA Modules:
  0.0 465.1 jit_solution(6829492691934465839)
XLA Ops:
  7.2 0.7 compare_select_fusion
  8.1 1.4 gather_fusion
  9.6 0.8 add_select_fusion.1
  10.7 0.8 fusion.21
  12.2 1.6 gather_fusion.1
  13.8 1.1 select_multiply_fusion.3
  15.0 6.8 %all-to-all-start = ((bf16[8,512,64]{1,2,0:T(8,128)(2,1)}), bf16[8,512,64]{1,2,0:T(8,128)(2,1)S(1)}, u32[]{:S(2)}, u32[]{:S(2)}) async-start(bf16[8,512,64]{1,2,0:T(8,128)(2,1)} %get-tuple-element.14), calls=%async_computation | async-start | bytes 1048576 | tf_op jit(solution)/shard_map/all_to_all | solution.py:76
  22.0 9.1 %all-to-all-done = bf16[8,512,64]{1,2,0:T(8,128)(2,1)S(1)} async-done(((bf16[8,512,64]{1,2,0:T(8,128)(2,1)}), bf16[8,512,64]{1,2,0:T(8,128)(2,1)S(1)}, u32[]{:S(2)}, u32[]{:S(2)}) %all-to-all-start) | async-done | bytes 524320 | tf_op jit(solution)/shard_map/all_to_all | solution.py:76
  31.1 4.4 all-to-all-start.2
  36.2 8.7 %all-to-all-done.2 = bf16[8,512,64]{1,2,0:T(8,128)(2,1)S(1)} async-done(((bf16[8,512,64]{1,2,0:T(8,128)(2,1)}), bf16[8,512,64]{1,2,0:T(8,128)(2,1)S(1)}, u32[]{:S(2)}, u32[]{:S(2)}) %all-to-all-start.2) | async-done | bytes 524320 | tf_op jit(solution)/shard_map/all_to_all | solution.py:78
  46.6 0.8 multiply_reduce_fusion
  47.4 0.7 all-gather.2.cloned.1.call-update
  48.1 0.6 gather_fusion.7
  48.7 1.6 gather_fusion.3
  50.3 1.0 select_multiply_fusion
  51.3 12.7 %all_to_all.20 = bf16[8,64,512]{2,1,0:T(8,128)(2,1)S(1)} all-to-all(bf16[8,64,512]{2,1,0:T(8,128)(2,1)S(1)} %get-tuple-element.12), channel_id=1, replica_groups=mesh['group'=8,'tensor'=16] {'group'}, dimensions={0} | all-to-all | bytes 1048576 | tf_op jit(solution)/shard_map/all_to_all | solution.py:79
  64.0 4.4 all-to-all-start.1
  68.4 9.8 %fusion.32 = f32[384,8192]{1,0:T(8,128)} fusion(bf16[384,512]{1,0:T(8,128)(2,1)S(1)} %copy-done.1, bf16[512,8192]{1,0:T(8,128)(2,1)} %param.19), kind=kOutput, calls=%fused_computation.76 | convolution fusion | flops 3221225472 | bytes 21364736 | tf_op jit(solution)/shard_map/dot_general | solution.py:99
  79.4 50.0 %all-reduce.4.cloned.1.call-done = (f32[384,64]{0,1:T(8,128)}, f32[384,64]{0,1:T(8,128)}) async-done(((f32[384,64]{0,1:T(8,128)}, f32[384,64]{0,1:T(8,128)}), (f32[384,64]{0,1:T(8,128)}, f32[384,64]{0,1:T(8,128)})) %all-reduce.4.cloned.1.call-update) | async-done | bytes 196624 | tf_op jit(solution)/shard_map/psum | solution.py:92
  129.4 3.0 fusion.4
  132.4 277.3 %all-reduce.5 = bf16[384,8192]{1,0:T(8,128)(2,1)} all-reduce(f32[384,8192]{1,0:T(8,128)} %fusion.4), channel_id=1, replica_groups=mesh['group'=8,'tensor'=16] {'tensor'}, use_global_device_ids=true, to_apply=%region_9.12 | all-reduce | flops 3145728 | bytes 18874368 | tf_op jit(solution)/shard_map/psum | solution.py:105
  409.7 39.2 %all-gather.2.cloned.1.call-done = bf16[384,8192]{1,0:T(8,128)(2,1)} async-done(((bf16[384,512]{1,0:T(8,128)(2,1)}), bf16[384,8192]{1,0:T(8,128)(2,1)}) %all-gather.2.cloned.1.call-update) | async-done | bytes 6291472 | tf_op jit(solution)/shard_map/all_gather | solution.py:94
  448.9 7.7 %fusion.30 = f32[384,512]{1,0:T(8,128)S(1)} fusion(bf16[384,8192]{1,0:T(8,128)(2,1)} %all-gather.2.cloned.1.call-done, bf16[8192,512]{1,0:T(8,128)(2,1)} %param.18), kind=kOutput, calls=%fused_computation.74 | convolution fusion | flops 3221225472 | bytes 15466496 | tf_op jit(solution)/shard_map/dot_general | solution.py:93
  456.6 1.6 fusion.5
  (44 shorter events, 5.0 us)
Async XLA Ops:
  7.2 4.4 copy-start
  7.2 14.6 %copy-start.4 = (s32[1,16]{1,0:T(1,128)S(1)}, s32[1,16]{1,0:T(1,128)}, u32[]{:S(2)}) copy-start(s32[1,16]{1,0:T(1,128)} %param.23) | copy-start | bytes 196
  7.2 28.3 %copy-start.5 = (s32[1,16]{1,0:T(1,128)S(1)}, s32[1,16]{1,0:T(1,128)}, u32[]{:S(2)}) copy-start(s32[1,16]{1,0:T(1,128)} %param.22) | copy-start | bytes 196
  9.5 36.1 %copy-start.1 = (bf16[384,512]{1,0:T(8,128)(2,1)S(1)}, bf16[384,512]{1,0:T(8,128)(2,1)}, u32[]{:S(2)}) copy-start(bf16[384,512]{1,0:T(8,128)(2,1)} %param.17) | copy-start | bytes 1179652
  9.5 36.6 %copy-start.2 = (bf16[384,512]{1,0:T(8,128)(2,1)S(1)}, bf16[384,512]{1,0:T(8,128)(2,1)}, u32[]{:S(2)}) copy-start(bf16[384,512]{1,0:T(8,128)(2,1)} %param.16) | copy-start | bytes 1179652
  13.8 34.3 %copy-start.3 = (bf16[8,64,512]{2,1,0:T(8,128)(2,1)S(1)}, bf16[8,64,512]{2,1,0:T(8,128)(2,1)}, u32[]{:S(2)}) copy-start(bf16[8,64,512]{2,1,0:T(8,128)(2,1)} %param.27) | copy-start | bytes 1572868
  15.0 16.2 %all-to-all-start = ((bf16[8,512,64]{1,2,0:T(8,128)(2,1)}), bf16[8,512,64]{1,2,0:T(8,128)(2,1)S(1)}, u32[]{:S(2)}, u32[]{:S(2)}) async-start(bf16[8,512,64]{1,2,0:T(8,128)(2,1)} %get-tuple-element.14), calls=%async_computation | async-start | bytes 1048576 | tf_op jit(solution)/shard_map/all_to_all | solution.py:76
  31.1 13.7 %all-to-all-start.2 = ((bf16[8,512,64]{1,2,0:T(8,128)(2,1)}), bf16[8,512,64]{1,2,0:T(8,128)(2,1)S(1)}, u32[]{:S(2)}, u32[]{:S(2)}) async-start(bf16[8,512,64]{1,2,0:T(8,128)(2,1)} %get-tuple-element.15), calls=%async_computation.2 | async-start | bytes 1048576 | tf_op jit(solution)/shard_map/all_to_all | solution.py:78
  35.5 93.9 %all-reduce.4.cloned.1.call-start = ((), (), s32[]{:S(2)}) async-start(), calls=%async_computation.5 | async-start | bytes 393216 | tf_op jit(solution)/shard_map/psum | solution.py:92
  47.4 401.5 %all-gather.2.cloned.1.call-start = ((), (), s32[]{:S(2)}) async-start(), calls=%async_computation.4 | async-start | bytes 6684672 | tf_op jit(solution)/shard_map/all_gather | solution.py:94
  64.0 14.8 %all-to-all-start.1 = ((bf16[8,64,512]{2,1,0:T(8,128)(2,1)}), bf16[8,64,512]{2,1,0:T(8,128)(2,1)S(1)}, u32[]{:S(2)}, u32[]{:S(2)}) async-start(bf16[8,64,512]{2,1,0:T(8,128)(2,1)} %get-tuple-element.13), calls=%async_computation.1 | async-start | bytes 1048576 | tf_op jit(solution)/shard_map/all_to_all | solution.py:77
  409.7 47.0 %copy-start.6 = (f32[384,64]{0,1:T(8,128)S(1)}, f32[384,64]{0,1:T(8,128)}, u32[]{:S(2)}) copy-start(f32[384,64]{0,1:T(8,128)} %get-tuple-element.6) | copy-start | bytes 294916
Sparse Core Ops, SparseCore 0:
  47.5 81.8 all-reduce.3
  131.5 317.2 all-gather.1
where the time goes:
time: 466 us; the launch traced here: 465 us
  blocking collectives  290 us (62%)
  waiting for transfers between devices  108 us (23%)
  matrix products  23 us (5%)
  starting transfers between devices  15.6 us (3%)
  between operations  14.3 us (3%)
  local copies, waits for them, and re-layouts  8.43 us (2%)
  other arithmetic  6.07 us (1%)
    psum x1, blocking collectives, body(): attn_out = lax.psum(o_term, 'tensor').astype(jnp.bfloat16)  277 us
    psum x1, waiting for transfers between devices, body(): q_down, o_down = lax.psum((q_partial, output_partial_sum), 'tensor')  50 us
    all_gather x1, waiting for transfers between devices, body(): lax.all_gather(hidden_rows, 'tensor', axis=1, tiled=True)  39.2 us
    all_to_all x1, blocking collectives, body(): lax.all_to_all(pack(ob_store), 'group', split_axis=0, concat_axis=0, tile...  12.7 us
    dot_general x1, matrix products, body(): o_term = jnp.dot(attn_rows, o_weight, preferred_element_type=jnp.float32)  9.77 us
  transfers between devices with their start and end apart: 5, of which 4 were waited for; matrix products, arithmetic and copies ran while one was open for 4% of the time, Pallas kernels for 0%

commit v1 on v0

v1 whole, which is shorter than its diff:
```python
import jax
import jax.numpy as jnp
from jax import lax
from jax.experimental import pallas as pl
from jax.experimental.pallas import tpu as pltpu
from jax.sharding import PartitionSpec as P

MESH = pl.DeviceIdType.MESH
F32 = jnp.float32
BF16 = jnp.bfloat16

W_Y = 0
W_Z = 6
W_SIB = 18
ATT = 30
ADP_A = 34
ADP_B = 42
DOWN_1 = 50
DOWN_2 = 53
DOWN_3 = 56
RED = 59
HID = 65
OUT = 105
N_SEMS = 145
N_LOCAL = 12


def mod(a, n):
    return lax.rem(a + n, n)


def kernel(
    hidden, attn, q_weight, o_weight, qa, qb, oa, ob, table, adapters, req_slot, req_len,
    q_out, a_out,
    hid_all, attn_all, w_o, w_stage, w_q, qa_v, qb_v, oa_v, ob_v, send_a, send_b, recv_a, recv_b,
    owner_v, down_v, down_1, down_2, down_s, down_all, up_q, up_o, part, r_opp, r_nbr, o_blk, q_blk,
    send_sem, recv_sem, local_sem,
):
    g = lax.axis_index("group")
    t = lax.axis_index("tensor")
    z, c = lax.div(g, 2), lax.rem(g, 2)
    y, x = lax.div(t, 4), lax.rem(t, 4)
    ys = [y, mod(y - 1, 4), mod(y + 1, 4), mod(y + 2, 4)]
    xs = [x, mod(x - 1, 4), mod(x + 1, 4), mod(x + 2, 4)]
    gs = [g] + [mod(z + d, 4) * 2 + c for d in (-1, 1, 2)]
    sib = z * 2 + (1 - c)
    gsib = [sib] + [mod(z + d, 4) * 2 + (1 - c) for d in (-1, 1, 2)]
    dev_x = [None] + [{"tensor": y * 4 + xs[i]} for i in (1, 2, 3)]
    dev_y = [None] + [{"tensor": ys[i] * 4 + x} for i in (1, 2, 3)]
    dev_z = [None] + [{"group": gs[i]} for i in (1, 2)]
    dev_sib = {"group": sib}

    sent = []

    def send(k, src, dst, dev):
        copy = pltpu.make_async_remote_copy(
            src_ref=src, dst_ref=dst, send_sem=send_sem.at[k], recv_sem=recv_sem.at[k],
            device_id=dev, device_id_type=MESH,
        )
        copy.start()
        sent.append(copy)

    def got(k, ref):
        pltpu.make_async_remote_copy(
            src_ref=ref, dst_ref=ref, send_sem=send_sem.at[k], recv_sem=recv_sem.at[k],
            device_id=dev_sib, device_id_type=MESH,
        ).wait_recv()

    def load(k, src, dst):
        copy = pltpu.make_async_copy(src, dst, local_sem.at[k])
        copy.start()
        return copy

    barrier = pltpu.get_barrier_semaphore()
    for i in (1, 2, 3):
        pl.semaphore_signal(barrier, inc=1, device_id=dev_x[i], device_id_type=MESH)
        pl.semaphore_signal(barrier, inc=1, device_id=dev_y[i], device_id_type=MESH)
    for d in range(1, 8):
        pl.semaphore_signal(barrier, inc=1, device_id={"group": mod(g + d, 8)}, device_id_type=MESH)
    col_y = [pl.multiple_of(v * 2048, 2048) for v in ys]
    l_qa, l_oa = load(0, qa, qa_v), load(1, oa, oa_v)
    l_qb, l_ob = load(2, qb, qb_v), load(3, ob, ob_v)
    l_attn = load(4, attn, attn_all.at[y])
    l_hid = load(5, hidden, hid_all.at[t])
    l_wo = load(6, o_weight.at[:, pl.ds(col_y[0], 2048)], w_o.at[y])
    l_wq = load(7, q_weight, w_q)
    pl.semaphore_wait(barrier, 13)

    class Gather:
        def __init__(self, base, buf, own):
            self.base, self.buf, self.own = base, buf, own

        def block(self, half, i, j):
            return ys[j] * 4 + xs[i] if half == 0 else ys[i] * 4 + xs[j]

        def devs(self, half):
            return (dev_x, dev_y) if half == 0 else (dev_y, dev_x)

        def rows(self, half, i, j, quarter=None):
            b = self.block(half, i, j)
            if quarter is None:
                return self.buf.at[b, pl.ds(half * 192, 192)]
            return self.buf.at[b, pl.ds(half * 192 + quarter * 96, 96)]

        def src_own(self, half):
            return self.own.at[pl.ds(half * 192, 192)]

        def first_own(self, half):
            dev = self.devs(half)[0]
            k = self.base + half * 20
            send(k, self.src_own(half), self.rows(half, 0, 0), dev[2])
            send(k + 1, self.src_own(half), self.rows(half, 0, 0), dev[1])

        def first_fwd(self, half):
            dev = self.devs(half)[0]
            k = self.base + half * 20
            got(k, self.rows(half, 1, 0))
            send(k + 2, self.rows(half, 1, 0, 0), self.rows(half, 1, 0, 0), dev[2])
            got(k + 1, self.rows(half, 2, 0))
            send(k + 3, self.rows(half, 2, 0, 1), self.rows(half, 2, 0, 1), dev[1])

        def first_opp(self, half):
            k = self.base + half * 20
            got(k + 2, self.rows(half, 3, 0, 0))
            got(k + 3, self.rows(half, 3, 0, 1))

        def second_own(self, half, i):
            dev = self.devs(half)[1]
            k = self.base + half * 20 + 4 + 4 * i
            src = self.src_own(half) if i == 0 else self.rows(half, i, 0)
            send(k, src, self.rows(half, i, 0), dev[2])
            send(k + 1, src, self.rows(half, i, 0), dev[1])

        def second_fwd(self, half, i):
            dev = self.devs(half)[1]
            k = self.base + half * 20 + 4 + 4 * i
            got(k, self.rows(half, i, 1))
            send(k + 2, self.rows(half, i, 1, 0), self.rows(half, i, 1, 0), dev[2])
            got(k + 1, self.rows(half, i, 2))
            send(k + 3, self.rows(half, i, 2, 1), self.rows(half, i, 2, 1), dev[1])

        def second_opp(self, half, i):
            k = self.base + half * 20 + 4 + 4 * i
            got(k + 2, self.rows(half, i, 3, 0))
            got(k + 3, self.rows(half, i, 3, 1))

    hid = Gather(HID, hid_all, hidden)
    out = Gather(OUT, a_out, o_blk)

    def wrows(i, grp, half=None):
        if half is None:
            return w_o.at[ys[i], pl.ds(pl.multiple_of(grp * 64, 64), 64)]
        return w_o.at[ys[i], pl.ds(pl.multiple_of(grp * 64 + half * 32, 32), 32)]

    row_g = pl.multiple_of(g * 64, 64)
    send(W_Y, o_weight.at[pl.ds(row_g, 64), pl.ds(col_y[2], 2048)], wrows(0, g), dev_y[2])
    send(W_Y + 1, o_weight.at[pl.ds(row_g, 64), pl.ds(col_y[1], 2048)], wrows(0, g), dev_y[1])
    hid.first_own(0)
    send(W_Y + 2, o_weight.at[pl.ds(row_g, 32), pl.ds(col_y[3], 2048)], w_stage.at[0], dev_y[2])
    send(
        W_Y + 3,
        o_weight.at[pl.ds(pl.multiple_of(g * 64 + 32, 32), 32), pl.ds(col_y[3], 2048)],
        w_stage.at[1],
        dev_y[1],
    )
    hid.first_own(1)
    hid.second_own(1, 0)

    def w_spread(i):
        send(W_Z + 4 * i, wrows(i + 1, g), wrows(i + 1, g), dev_z[2])
        send(W_Z + 4 * i + 1, wrows(i + 1, g), wrows(i + 1, g), dev_z[1])
        send(W_SIB + 4 * i, wrows(i + 1, g), wrows(i + 1, g), dev_sib)

    def w_pass(i):
        got(W_Z + 4 * i, wrows(i + 1, gs[1]))
        send(W_Z + 4 * i + 2, wrows(i + 1, gs[1], 0), wrows(i + 1, gs[1], 0), dev_z[2])
        got(W_Z + 4 * i + 1, wrows(i + 1, gs[2]))
        send(W_Z + 4 * i + 3, wrows(i + 1, gs[2], 1), wrows(i + 1, gs[2], 1), dev_z[1])
        for s in (1, 2):
            send(W_SIB + 4 * i + s, wrows(i + 1, gs[s]), wrows(i + 1, gs[s]), dev_sib)

    def w_last(i):
        got(W_Z + 4 * i + 2, wrows(i + 1, gs[3], 0))
        got(W_Z + 4 * i + 3, wrows(i + 1, gs[3], 1))
        send(W_SIB + 4 * i + 3, wrows(i + 1, gs[3]), wrows(i + 1, gs[3]), dev_sib)

    l_qa.wait()
    l_oa.wait()
    l_qb.wait()
    l_ob.wait()

    def local_index(dest):
        def body(s, found):
            place = table[adapters[dest, s]]
            return jnp.where(lax.div(place, 8) == g, lax.rem(place, 8), found)

        return lax.fori_loop(0, 8, body, jnp.int32(0))

    def pack(d, carry):
        idx = local_index(mod(g + d, 8))
        send_a[d, :, 0:64] = qa_v[idx]
        send_a[d, :, 64:128] = oa_v[idx]
        send_b[d, 0:64, :] = qb_v[idx]
        send_b[d, 64:128, :] = ob_v[idx]
        return carry

    lax.fori_loop(0, 8, pack, 0)
    recv_a[g] = send_a[0]
    recv_b[g] = send_b[0]

    row = lax.broadcasted_iota(jnp.int32, (384, 128), 0)
    owner_v[...] = jnp.zeros((384, 128), jnp.int32)

    def mark(k, start):
        end = start + req_len[0, k]
        own = lax.div(table[adapters[g, req_slot[0, k]]], 8)
        owner_v[...] = jnp.where((row >= start) & (row < end), own, owner_v[...])
        return end

    lax.fori_loop(0, 16, mark, jnp.int32(0))

    hid.first_fwd(0)
    got(W_Y, wrows(1, g))
    w_spread(0)
    got(W_Y + 1, wrows(2, g))
    w_spread(1)
    got(W_Y + 2, w_stage.at[0])
    send(W_Y + 4, w_stage.at[0], wrows(1, g, 0), dev_y[2])
    got(W_Y + 3, w_stage.at[1])
    send(W_Y + 5, w_stage.at[1], wrows(2, g, 1), dev_y[1])
    l_attn.wait()
    send(ATT, attn, attn_all.at[y], dev_y[2])
    send(ATT + 1, attn, attn_all.at[y], dev_y[1])
    hid.first_fwd(1)
    hid.second_own(1, 1)
    hid.second_own(1, 2)
    hid.second_fwd(1, 0)
    w_pass(0)
    got(W_Y + 4, wrows(3, g, 0))
    got(W_Y + 5, wrows(3, g, 1))
    w_spread(2)
    w_pass(1)
    hid.second_fwd(1, 1)
    hid.second_fwd(1, 2)
    got(ATT, attn_all.at[ys[1]])
    send(ATT + 2, attn_all.at[ys[1], pl.ds(0, 192)], attn_all.at[ys[1], pl.ds(0, 192)], dev_y[2])
    got(ATT + 1, attn_all.at[ys[2]])
    send(ATT + 3, attn_all.at[ys[2], pl.ds(192, 192)], attn_all.at[ys[2], pl.ds(192, 192)], dev_y[1])
    hid.first_opp(1)
    hid.second_own(1, 3)
    hid.second_own(0, 0)
    hid.second_own(0, 1)
    hid.second_own(0, 2)
    hid.first_opp(0)
    hid.second_own(0, 3)
    w_last(0)
    w_pass(2)
    for d in range(1, 8):
        send(ADP_A + d, send_a.at[d], recv_a.at[g], {"group": mod(g + d, 8)})
    for d in range(1, 8):
        send(ADP_B + d, send_b.at[d], recv_b.at[g], {"group": mod(g + d, 8)})
    w_last(1)
    w_last(2)

    l_wo.wait()
    got(ATT + 2, attn_all.at[ys[3], pl.ds(0, 192)])
    got(ATT + 3, attn_all.at[ys[3], pl.ds(192, 192)])
    for i in range(3):
        for s in range(4):
            got(W_SIB + 4 * i + s, wrows(i + 1, gsib[s]))

    def partial(slot, xi):
        cols = pl.ds(pl.multiple_of(xs[xi] * 512, 512), 512)

        def half(h, carry):
            rows = pl.ds(pl.multiple_of(h * 192, 192), 192)
            total = jnp.dot(attn_all[0, rows, :], w_o[0, :, cols], preferred_element_type=F32)
            for i in range(1, 4):
                total = total + jnp.dot(attn_all[i, rows, :], w_o[i, :, cols], preferred_element_type=F32)
            part[slot, rows, :] = total
            return carry

        lax.fori_loop(0, 2, half, 0)

    upper, lower = pl.ds(0, 192), pl.ds(192, 192)
    partial(0, 3)
    send(RED, part.at[0, upper], r_opp.at[0], dev_x[2])
    send(RED + 1, part.at[0, lower], r_opp.at[1], dev_x[1])
    partial(1, 2)
    send(RED + 2, part.at[1, lower], r_nbr.at[0, lower], dev_x[2])
    partial(2, 1)
    send(RED + 3, part.at[2, upper], r_nbr.at[1, upper], dev_x[1])
    partial(3, 0)
    for i in range(4):
        hid.second_fwd(0, i)
    hid.second_fwd(1, 3)
    got(RED, r_opp.at[0])
    part[1, upper, :] = part[1, upper, :] + r_opp[0]
    send(RED + 4, part.at[1, upper], r_nbr.at[0, upper], dev_x[2])
    got(RED + 1, r_opp.at[1])
    part[2, lower, :] = part[2, lower, :] + r_opp[1]
    send(RED + 5, part.at[2, lower], r_nbr.at[1, lower], dev_x[1])

    l_hid.wait()
    for d in range(1, 8):
        got(ADP_A + d, recv_a.at[mod(g - d + 8, 8)])
    lane = lax.broadcasted_iota(jnp.int32, (384, 128), 1)
    down_v[...] = jnp.zeros((384, 128), F32)

    def down(o, carry):
        a = recv_a[o]
        from_hid = jnp.dot(hid_all[t], a, preferred_element_type=F32)
        from_att = jnp.dot(attn_all[y], a, preferred_element_type=F32)
        value = jnp.where(lane < 64, from_hid, from_att)
        down_v[...] = jnp.where(owner_v[...] == o, value, down_v[...])
        return carry

    lax.fori_loop(0, 8, down, 0)

    def piece(v):
        return pl.ds(pl.multiple_of(v * 96, 32), 96)

    y_off = [mod(y + d, 4) for d in range(4)]
    y_back = [mod(y - d + 4, 4) for d in range(4)]
    for d in (1, 2, 3):
        send(DOWN_1 + d - 1, down_v.at[piece(y_off[d])], down_1.at[d - 1], {"tensor": y_off[d] * 4 + x})
    for d in (1, 2, 3):
        got(DOWN_1 + d - 1, down_1.at[d - 1])
    down_s[0] = down_v[piece(y), :] + down_1[0] + down_1[1] + down_1[2]
    for d in (1, 2, 3):
        send(DOWN_2 + d - 1, down_s.at[0], down_2.at[d - 1], {"tensor": y * 4 + mod(x + d, 4)})
    for d in (1, 2, 3):
        got(DOWN_2 + d - 1, down_2.at[d - 1])
    down_s[1] = down_s[0] + down_2[0] + down_2[1] + down_2[2]
    for d in (1, 2, 3):
        send(DOWN_3 + d - 1, down_s.at[1], down_all.at[piece(y)], {"tensor": y_off[d] * 4 + x})
    down_all[piece(y), :] = down_s[1]
    for d in (1, 2, 3):
        got(DOWN_3 + d - 1, down_all.at[piece(y_back[d])])

    for d in range(1, 8):
        got(ADP_B + d, recv_b.at[mod(g - d + 8, 8)])
    up_q[...] = jnp.zeros((384, 512), F32)
    up_o[...] = jnp.zeros((384, 512), F32)

    def up(o, carry):
        b = recv_b[o]
        rows = jnp.where(owner_v[...] == o, down_all[...] * 0.5, 0.0)
        for keep, total in ((lane < 64, up_q), (lane >= 64, up_o)):
            kept = jnp.where(keep, rows, 0.0)
            high = kept.astype(BF16)
            low = (kept - high.astype(F32)).astype(BF16)
            total[...] += jnp.dot(high, b, preferred_element_type=F32) + jnp.dot(low, b, preferred_element_type=F32)
        return carry

    lax.fori_loop(0, 8, up, 0)
    part[3] = part[3] + up_o[...]

    for i in range(4):
        hid.second_opp(0, i)
        hid.second_opp(1, i)
    l_wq.wait()

    def query(k, carry):
        rows = pl.ds(pl.multiple_of(k * 512, 512), 512)
        up_q[...] += jnp.dot(hid_all[k], w_q[rows, :], preferred_element_type=F32)
        return carry

    lax.fori_loop(0, 16, query, 0)
    q_blk[...] = up_q[...].astype(BF16)
    s_q = load(8, q_blk, q_out)

    got(RED + 2, r_nbr.at[0, lower])
    got(RED + 3, r_nbr.at[1, upper])
    got(RED + 4, r_nbr.at[0, upper])
    got(RED + 5, r_nbr.at[1, lower])
    o_blk[...] = (part[3] + r_nbr[0] + r_nbr[1]).astype(BF16)
    s_o = load(9, o_blk, a_out.at[t])
    out.first_own(0)
    out.first_own(1)
    out.second_own(1, 0)
    out.second_own(0, 0)
    out.first_fwd(0)
    out.first_fwd(1)
    for i in (1, 2):
        out.second_own(0, i)
        out.second_own(1, i)
    out.second_fwd(0, 0)
    out.second_fwd(1, 0)
    out.first_opp(0)
    out.second_own(0, 3)
    out.first_opp(1)
    out.second_own(1, 3)
    for i in (1, 2, 3):
        out.second_fwd(0, i)
        out.second_fwd(1, i)
    for i in range(4):
        out.second_opp(0, i)
        out.second_opp(1, i)
    for copy in sent:
        copy.wait_send()
    s_q.wait()
    s_o.wait()


def body(hidden, attn, q_weight, o_weight, table, adapters, req_slot, req_len, qa, qb, oa, ob):
    hbm = pl.BlockSpec(memory_space=pl.ANY)
    smem = pl.BlockSpec(memory_space=pltpu.SMEM)
    vm = pltpu.VMEM
    queries, blocks = pl.pallas_call(
        kernel,
        out_shape=(
            jax.ShapeDtypeStruct((384, 512), BF16),
            jax.ShapeDtypeStruct((16, 384, 512), BF16),
        ),
        in_specs=[hbm] * 8 + [smem] * 4,
        out_specs=(hbm, hbm),
        scratch_shapes=[
            vm((16, 384, 512), BF16),
            vm((4, 384, 512), BF16),
            vm((4, 512, 2048), BF16),
            vm((2, 32, 2048), BF16),
            vm((8192, 512), BF16),
            vm((8, 512, 64), BF16),
            vm((8, 64, 512), BF16),
            vm((8, 512, 64), BF16),
            vm((8, 64, 512), BF16),
            vm((8, 512, 128), BF16),
            vm((8, 128, 512), BF16),
            vm((8, 512, 128), BF16),
            vm((8, 128, 512), BF16),
            vm((384, 128), jnp.int32),
            vm((384, 128), F32),
            vm((3, 96, 128), F32),
            vm((3, 96, 128), F32),
            vm((2, 96, 128), F32),
            vm((384, 128), F32),
            vm((384, 512), F32),
            vm((384, 512), F32),
            vm((4, 384, 512), F32),
            vm((2, 192, 512), F32),
            vm((2, 384, 512), F32),
            vm((384, 512), BF16),
            vm((384, 512), BF16),
            pltpu.SemaphoreType.DMA((N_SEMS,)),
            pltpu.SemaphoreType.DMA((N_SEMS,)),
            pltpu.SemaphoreType.DMA((N_LOCAL,)),
        ],
        compiler_params=pltpu.CompilerParams(
            collective_id=0, has_side_effects=True, vmem_limit_bytes=60 * 1024 * 1024
        ),
    )(hidden, attn, q_weight, o_weight, qa, qb, oa, ob, table, adapters, req_slot, req_len)
    return queries, jnp.transpose(blocks, (1, 0, 2)).reshape(384, 8192)


def solution(mesh):
    return jax.shard_map(
        body,
        mesh=mesh,
        in_specs=(
            P("group", "tensor"),
            P("group", "tensor"),
            P(None, "tensor"),
            P("tensor", None),
            P(),
            P(),
            P("group", None),
            P("group", None),
            P("group", "tensor", None),
            P("group", None, "tensor"),
            P("group", "tensor", None),
            P("group", None, "tensor"),
        ),
        out_specs=(P("group", "tensor"), P("group", None)),
        check_vma=False,
    )
```

time: 466 us -> 158 us (0.34)
  blocking collectives: 290 us -> 0 us
  Pallas kernels: 0 us -> 131 us
  waiting for transfers between devices: 108 us -> 0 us
  matrix products: 23 us -> 0 us
  starting transfers between devices: 15.6 us -> 0 us
  local copies, waits for them, and re-layouts: 8.43 us -> 22.8 us
  between operations: 14.3 us -> 0.64 us
  other arithmetic: 6.07 us -> 0 us
    psum x1 -> x0, blocking collectives: 277 us -> none  [body(): attn_out = lax.psum(o_term, 'tensor').astype(jnp.bfloat16)]
    pallas_call x0 -> x1, Pallas kernels: none -> 131 us  [body(): pl.pallas_call(kernel, out_shape=(jax.ShapeDtypeStruct((384, 512), BF16),...]
    psum x1 -> x0, waiting for transfers between devices: 50 us -> none  [body(): q_down, o_down = lax.psum((q_partial, output_partial_sum), 'tensor')]
    all_gather x1 -> x0, waiting for transfers between devices: 39.2 us -> none  [body(): lax.all_gather(hidden_rows, 'tensor', axis=1, tiled=True)]
    dot_general x6 -> x0, matrix products: 23 us -> none  [the longest x1 9.77 us: body(): o_term = jnp.dot(attn_rows, o_weight, preferred_element_type=jnp.float32)]
    all_to_all x3 -> x0, waiting for transfers between devices: 17.8 us -> none  [the longest x1 9.1 us: body(): lax.all_to_all(pack(qa_store), 'group', split_axis=0, concat_axis=0, tile...]
    all_to_all x3 -> x0, starting transfers between devices: 15.6 us -> none  [the longest x1 6.8 us: body(): lax.all_to_all(pack(qa_store), 'group', split_axis=0, concat_axis=0, tile...]
    unnamed x14 -> x6, local copies, waits for them, and re-layouts: 0.04 us -> 14.1 us
  transfers between devices with their start and end apart: 5 -> 0, of which waited for: 4 -> 0; matrix products, arithmetic and copies ran while one was open for 4% -> 0% of each run, Pallas kernels for 0% -> 0%
where the time goes in v1:
time: 158 us; the launch traced here: 155 us
  Pallas kernels  131 us (83%)
  local copies, waits for them, and re-layouts  22.8 us (14%)
    pallas_call x1, Pallas kernels, body(): pl.pallas_call(kernel, out_shape=(jax.ShapeDtypeStruct((384, 512), BF16),...  131 us
    unnamed x6, local copies, waits for them, and re-layouts  14.1 us
    transpose x1, local copies, waits for them, and re-layouts, body(): return (queries, jnp.transpose(blocks, (1, 0, 2)).reshape(384, 8192))  8.64 us

profile of v1, /device:TPU:1, one launch (start us, length us, event | category | flops | bytes accessed | tf_op | source)
XLA Modules:
  0.0 154.6 jit_solution(15574484732742440554)
XLA Ops:
  0.6 2.4 %copy.16.qa = bf16[8,512,64]{2,1,0:T(8,128)(2,1)} copy(bf16[8,512,64]{1,2,0:T(8,128)(2,1)} %param.20) | data formatting | bytes 1048576 | tf_op args[8]
  3.0 2.4 %copy.17.oa = bf16[8,512,64]{2,1,0:T(8,128)(2,1)} copy(bf16[8,512,64]{1,2,0:T(8,128)(2,1)} %param.22) | data formatting | bytes 1048576 | tf_op args[10]
  5.4 131.2 %shard_map.131 = (bf16[384,512]{1,0:T(8,128)(2,1)}, bf16[16,384,512]{2,1,0:T(8,128)(2,1)}) custom-call(bf16[384,512]{1,0:T(8,128)(2,1)} %hidden.1, bf16[384,512]{1,0:T(8,128)(2,1)} %attn.1, bf16[8192,512]{1,0:T(8,128)(2,1)} %q_weight.1, bf16[512,8192]{1,0:T(8,128)(2,1)} %o_weight.1, bf16[8,512,64]{2,1,0:T(8,128)(2,1)} %copy.16.qa, bf16[8,64,512]{2,1,0:T(8,128)(2,1)} %qb.1, ...), custom_call_target="tpu_custom_call" | custom-call | tf_op jit(solution)/shard_map/pallas_call | solution.py:410
  136.5 8.6 %copy.18 = bf16[384,16,512]{0,2,1:T(8,128)(2,1)} copy(bf16[384,16,512]{2,0,1:T(8,128)(2,1)} %bitcast.3) | data formatting | bytes 12582912 | tf_op jit(solution)/shard_map/transpose | solution.py:453
  145.2 0.0 copy-start
  145.2 8.7 %copy.19 = bf16[384,8192]{1,0:T(8,128)(2,1)} copy(bf16[384,8192]{0,1:T(8,128)(2,1)} %bitcast.2) | data formatting | bytes 12582912
  153.9 0.0 copy-done
  153.9 0.7 copy.21
Async XLA Ops:
  145.2 8.7 %copy-start = (bf16[384,512]{1,0:T(8,128)(2,1)S(1)}, bf16[384,512]{1,0:T(8,128)(2,1)}, u32[]{:S(2)}) copy-start(bf16[384,512]{1,0:T(8,128)(2,1)} %get-tuple-element.10) | copy-start | bytes 1179652

commit v2 on v1

--- a/solution.py
+++ b/solution.py
@@ -13,16 +13,15 @@
 W_Z = 6
 W_SIB = 18
 ATT = 30
-ADP_A = 34
-ADP_B = 42
-DOWN_1 = 50
-DOWN_2 = 53
-DOWN_3 = 56
-RED = 59
-HID = 65
-OUT = 105
-N_SEMS = 145
-N_LOCAL = 12
+ADP = 34
+DOWN_1 = 42
+DOWN_2 = 45
+DOWN_3 = 48
+RED = 51
+HID = 57
+OUT = 97
+N_SEMS = 137
+N_LOCAL = 8
 
 
 def mod(a, n):
@@ -32,8 +31,8 @@
 def kernel(
     hidden, attn, q_weight, o_weight, qa, qb, oa, ob, table, adapters, req_slot, req_len,
     q_out, a_out,
-    hid_all, attn_all, w_o, w_stage, w_q, qa_v, qb_v, oa_v, ob_v, send_a, send_b, recv_a, recv_b,
-    owner_v, down_v, down_1, down_2, down_s, down_all, up_q, up_o, part, r_opp, r_nbr, o_blk, q_blk,
+    hid_all, attn_all, w_o, w_stage, w_q, qa_v, qb_v, oa_v, ob_v, send_a, recv_a,
+    owner_v, down_v, down_1, down_2, down_s, down_all, up_q, up_o, part, r_opp, r_nbr,
     send_sem, recv_sem, local_sem,
 ):
     g = lax.axis_index("group")
@@ -98,9 +97,10 @@
 
         def rows(self, half, i, j, quarter=None):
             b = self.block(half, i, j)
-            if quarter is None:
-                return self.buf.at[b, pl.ds(half * 192, 192)]
-            return self.buf.at[b, pl.ds(half * 192 + quarter * 96, 96)]
+            start, size = (half * 192, 192) if quarter is None else (half * 192 + quarter * 96, 96)
+            if len(self.buf.shape) == 3:
+                return self.buf.at[b, pl.ds(start, size)]
+            return self.buf.at[pl.ds(start, size), pl.ds(pl.multiple_of(b * 512, 512), 512)]
 
         def src_own(self, half):
             return self.own.at[pl.ds(half * 192, 192)]
@@ -145,7 +145,7 @@
             got(k + 3, self.rows(half, i, 3, 1))
 
     hid = Gather(HID, hid_all, hidden)
-    out = Gather(OUT, a_out, o_blk)
+    out = Gather(OUT, a_out, a_out.at[:, pl.ds(pl.multiple_of(t * 512, 512), 512)])
 
     def wrows(i, grp, half=None):
         if half is None:
@@ -198,15 +198,14 @@
 
     def pack(d, carry):
         idx = local_index(mod(g + d, 8))
-        send_a[d, :, 0:64] = qa_v[idx]
-        send_a[d, :, 64:128] = oa_v[idx]
-        send_b[d, 0:64, :] = qb_v[idx]
-        send_b[d, 64:128, :] = ob_v[idx]
+        send_a[d, 0:64, :] = qa_v[idx]
+        send_a[d, 64:128, :] = oa_v[idx]
+        send_a[d, 128:192, :] = qb_v[idx]
+        send_a[d, 192:256, :] = ob_v[idx]
         return carry
 
     lax.fori_loop(0, 8, pack, 0)
     recv_a[g] = send_a[0]
-    recv_b[g] = send_b[0]
 
     row = lax.broadcasted_iota(jnp.int32, (384, 128), 0)
     owner_v[...] = jnp.zeros((384, 128), jnp.int32)
@@ -256,9 +255,7 @@
     w_last(0)
     w_pass(2)
     for d in range(1, 8):
-        send(ADP_A + d, send_a.at[d], recv_a.at[g], {"group": mod(g + d, 8)})
-    for d in range(1, 8):
-        send(ADP_B + d, send_b.at[d], recv_b.at[g], {"group": mod(g + d, 8)})
+        send(ADP + d, send_a.at[d], recv_a.at[g], {"group": mod(g + d, 8)})
     w_last(1)
     w_last(2)
 
@@ -303,14 +300,14 @@
 
     l_hid.wait()
     for d in range(1, 8):
-        got(ADP_A + d, recv_a.at[mod(g - d + 8, 8)])
+        got(ADP + d, recv_a.at[mod(g - d + 8, 8)])
     lane = lax.broadcasted_iota(jnp.int32, (384, 128), 1)
     down_v[...] = jnp.zeros((384, 128), F32)
 
     def down(o, carry):
-        a = recv_a[o]
-        from_hid = jnp.dot(hid_all[t], a, preferred_element_type=F32)
-        from_att = jnp.dot(attn_all[y], a, preferred_element_type=F32)
+        a = recv_a[o, 0:128, :]
+        from_hid = lax.dot_general(hid_all[t], a, (((1,), (1,)), ((), ())), preferred_element_type=F32)
+        from_att = lax.dot_general(attn_all[y], a, (((1,), (1,)), ((), ())), preferred_element_type=F32)
         value = jnp.where(lane < 64, from_hid, from_att)
         down_v[...] = jnp.where(owner_v[...] == o, value, down_v[...])
         return carry
@@ -338,13 +335,11 @@
     for d in (1, 2, 3):
         got(DOWN_3 + d - 1, down_all.at[piece(y_back[d])])
 
-    for d in range(1, 8):
-        got(ADP_B + d, recv_b.at[mod(g - d + 8, 8)])
     up_q[...] = jnp.zeros((384, 512), F32)
     up_o[...] = jnp.zeros((384, 512), F32)
 
     def up(o, carry):
-        b = recv_b[o]
+        b = recv_a[o, 128:256, :]
         rows = jnp.where(owner_v[...] == o, down_all[...] * 0.5, 0.0)
         for keep, total in ((lane < 64, up_q), (lane >= 64, up_o)):
             kept = jnp.where(keep, rows, 0.0)
@@ -367,15 +362,14 @@
         return carry
 
     lax.fori_loop(0, 16, query, 0)
-    q_blk[...] = up_q[...].astype(BF16)
-    s_q = load(8, q_blk, q_out)
+    q_out[...] = up_q[...].astype(BF16)
 
     got(RED + 2, r_nbr.at[0, lower])
     got(RED + 3, r_nbr.at[1, upper])
     got(RED + 4, r_nbr.at[0, upper])
     got(RED + 5, r_nbr.at[1, lower])
-    o_blk[...] = (part[3] + r_nbr[0] + r_nbr[1]).astype(BF16)
-    s_o = load(9, o_blk, a_out.at[t])
+    own_cols = pl.ds(pl.multiple_of(t * 512, 512), 512)
+    a_out[:, own_cols] = (part[3] + r_nbr[0] + r_nbr[1]).astype(BF16)
     out.first_own(0)
     out.first_own(1)
     out.second_own(1, 0)
@@ -399,36 +393,33 @@
         out.second_opp(1, i)
     for copy in sent:
         copy.wait_send()
-    s_q.wait()
-    s_o.wait()
 
 
 def body(hidden, attn, q_weight, o_weight, table, adapters, req_slot, req_len, qa, qb, oa, ob):
     hbm = pl.BlockSpec(memory_space=pl.ANY)
     smem = pl.BlockSpec(memory_space=pltpu.SMEM)
     vm = pltpu.VMEM
-    queries, blocks = pl.pallas_call(
+    qa_t, oa_t = jnp.transpose(qa, (0, 2, 1)), jnp.transpose(oa, (0, 2, 1))
+    return pl.pallas_call(
         kernel,
         out_shape=(
-            jax.ShapeDtypeStruct((384, 512), BF16),
-            jax.ShapeDtypeStruct((16, 384, 512), BF16),
+            vm((384, 512), BF16),
+            vm((384, 8192), BF16),
         ),
         in_specs=[hbm] * 8 + [smem] * 4,
-        out_specs=(hbm, hbm),
+        out_specs=[pl.BlockSpec(memory_space=pltpu.VMEM)] * 2,
         scratch_shapes=[
             vm((16, 384, 512), BF16),
             vm((4, 384, 512), BF16),
             vm((4, 512, 2048), BF16),
             vm((2, 32, 2048), BF16),
             vm((8192, 512), BF16),
-            vm((8, 512, 64), BF16),
             vm((8, 64, 512), BF16),
-            vm((8, 512, 64), BF16),
             vm((8, 64, 512), BF16),
-            vm((8, 512, 128), BF16),
-            vm((8, 128, 512), BF16),
-            vm((8, 512, 128), BF16),
-            vm((8, 128, 512), BF16),
+            vm((8, 64, 512), BF16),
+            vm((8, 64, 512), BF16),
+            vm((8, 256, 512), BF16),
+            vm((8, 256, 512), BF16),
             vm((384, 128), jnp.int32),
             vm((384, 128), F32),
             vm((3, 96, 128), F32),
@@ -440,17 +431,14 @@
             vm((4, 384, 512), F32),
             vm((2, 192, 512), F32),
             vm((2, 384, 512), F32),
-            vm((384, 512), BF16),
-            vm((384, 512), BF16),
             pltpu.SemaphoreType.DMA((N_SEMS,)),
             pltpu.SemaphoreType.DMA((N_SEMS,)),
             pltpu.SemaphoreType.DMA((N_LOCAL,)),
         ],
         compiler_params=pltpu.CompilerParams(
-            collective_id=0, has_side_effects=True, vmem_limit_bytes=60 * 1024 * 1024
+            collective_id=0, has_side_effects=True, vmem_limit_bytes=48 * 1024 * 1024
         ),
-    )(hidden, attn, q_weight, o_weight, qa, qb, oa, ob, table, adapters, req_slot, req_len)
-    return queries, jnp.transpose(blocks, (1, 0, 2)).reshape(384, 8192)
+    )(hidden, attn, q_weight, o_weight, qa_t, qb, oa_t, ob, table, adapters, req_slot, req_len)
 
 
 def solution(mesh):

time: 158 us -> 143 us (0.905)
  the two profiles are of different devices: /device:TPU:1 before, /device:TPU:96 now
where the time goes in v2:
time: 143 us
  Pallas kernels  139 us (97%)
  local copies, waits for them, and re-layouts  3.45 us (2%)
    pallas_call x1, Pallas kernels, body(): pl.pallas_call(kernel, out_shape=(vm((384, 512), BF16), vm((384, 8192), B...  139 us
    unnamed x2, local copies, waits for them, and re-layouts  3.45 us

profile of v2, /device:TPU:96, one launch (start us, length us, event | category | flops | bytes accessed | tf_op | source)
XLA Modules:
  0.0 143.0 jit_solution(9689118821271699893)
XLA Ops:
  0.6 138.9 %shard_map.131 = (bf16[384,512]{1,0:T(8,128)(2,1)S(1)}, bf16[384,8192]{1,0:T(8,128)(2,1)S(1)}) custom-call(bf16[384,512]{1,0:T(8,128)(2,1)} %hidden.1, bf16[384,512]{1,0:T(8,128)(2,1)} %attn.1, bf16[8192,512]{1,0:T(8,128)(2,1)} %q_weight.1, bf16[512,8192]{1,0:T(8,128)(2,1)} %o_weight.1, bf16[8,64,512]{2,1,0:T(8,128)(2,1)} %bitcast.2, ...), custom_call_target="tpu_custom_call" | custom-call | tf_op jit(solution)/shard_map/pallas_call | solution.py:403
  139.5 0.7 copy.16
  140.3 2.7 %copy.17 = bf16[384,8192]{1,0:T(8,128)(2,1)} copy(bf16[384,8192]{1,0:T(8,128)(2,1)S(1)} %get-tuple-element.3) | data formatting | bytes 12582912

commit v3 on v0

v3 whole, which is shorter than its diff:
```python
import jax
import jax.numpy as jnp
from jax import lax
from jax.experimental import pallas as pl
from jax.experimental.pallas import tpu as pltpu
from jax.sharding import PartitionSpec as P

MESH = pl.DeviceIdType.MESH
F32 = jnp.float32
BF16 = jnp.bfloat16

N_RECV = 58
N_SEND = 4
N_LOCAL = 7


def mod(a, n):
    return lax.rem(a + n, n)


def kernel(
    hidden, attn, q_weight, o_weight, qa, qb, oa, ob, table, adapters, req_slot, req_len,
    q_out, a_out,
    hid_all, attn_all, w_o, w_stage, w_q, qa_v, qb_v, oa_v, ob_v, send_a, recv_a,
    owner_v, down_v, down_1, down_2, down_s, down_all, up_q, up_o, part, r_opp, r_nbr, o_blk, q_blk,
    send_sem, recv_sem, local_sem,
):
    g = lax.axis_index("group")
    t = lax.axis_index("tensor")
    z, c = lax.div(g, 2), lax.rem(g, 2)
    y, x = lax.div(t, 4), lax.rem(t, 4)
    ys = [y, mod(y - 1, 4), mod(y + 1, 4), mod(y + 2, 4)]
    xs = [x, mod(x - 1, 4), mod(x + 1, 4), mod(x + 2, 4)]
    gs = [g] + [mod(z + d, 4) * 2 + c for d in (-1, 1, 2)]
    sib = z * 2 + (1 - c)
    dev_x = [None] + [{"tensor": y * 4 + xs[i]} for i in (1, 2, 3)]
    dev_y = [None] + [{"tensor": ys[i] * 4 + x} for i in (1, 2, 3)]
    dev_z = [None] + [{"group": gs[i]} for i in (1, 2)]
    dev_sib = {"group": sib}

    names, expected, leaving = {}, {}, {}

    def size(ref):
        count = 1
        for extent in ref.shape:
            count *= extent
        return count * ref.dtype.itemsize

    def wait_bytes(sem, count):
        rows = w_q.at[pl.ds(0, count // 1024)]
        pltpu.make_async_copy(rows, rows, sem).wait()

    def send(name, lot, src, dst, dev):
        k = names.setdefault(name, len(names))
        pltpu.make_async_remote_copy(
            src_ref=src, dst_ref=dst, send_sem=send_sem.at[lot], recv_sem=recv_sem.at[k],
            device_id=dev, device_id_type=MESH,
        ).start()
        expected[name] = expected.get(name, 0) + size(src)
        leaving[lot] = leaving.get(lot, 0) + size(src)

    def got(name):
        wait_bytes(recv_sem.at[names[name]], expected.pop(name))

    def gone(lot):
        wait_bytes(send_sem.at[lot], leaving.pop(lot))

    def load(k, src, dst):
        pltpu.make_async_copy(src, dst, local_sem.at[k]).start()
        return size(src)

    def loaded(k, count):
        wait_bytes(local_sem.at[k], count)

    barrier = pltpu.get_barrier_semaphore()
    for i in (1, 2, 3):
        pl.semaphore_signal(barrier, inc=1, device_id=dev_x[i], device_id_type=MESH)
        pl.semaphore_signal(barrier, inc=1, device_id=dev_y[i], device_id_type=MESH)
    for d in range(1, 8):
        pl.semaphore_signal(barrier, inc=1, device_id={"group": mod(g + d, 8)}, device_id_type=MESH)
    l_adp = load(0, qa, qa_v) + load(0, oa, oa_v) + load(0, qb, qb_v) + load(0, ob, ob_v)
    l_hid = load(1, hidden, hid_all.at[t])
    l_attn = load(2, attn, attn_all.at[y])
    x_slot = [xs[3], xs[2], xs[1], xs[0]]

    def wcols(i, j):
        return pl.ds(pl.multiple_of(ys[i] * 2048 + x_slot[j] * 512, 512), 512)

    l_wo = sum(load(3, o_weight.at[:, wcols(0, j)], w_o.at[y, j]) for j in range(4))

    def local_index(dest):
        def body(s, found):
            place = table[adapters[dest, s]]
            return jnp.where(lax.div(place, 8) == g, lax.rem(place, 8), found)

        return lax.fori_loop(0, 8, body, jnp.int32(0))

    def pack_adapters():
        loaded(0, l_adp)

        def pack(d, carry):
            idx = local_index(mod(g + d, 8))
            send_a[d, 0:64, :] = qa_v[idx]
            send_a[d, 64:128, :] = oa_v[idx]
            send_a[d, 128:192, :] = qb_v[idx]
            send_a[d, 192:256, :] = ob_v[idx]
            return carry

        lax.fori_loop(0, 8, pack, 0)
        recv_a[g] = send_a[0]

    def mark_rows():
        row = lax.broadcasted_iota(jnp.int32, (384, 128), 0)
        owner_v[...] = jnp.zeros((384, 128), jnp.int32)

        def mark(k, start):
            end = start + req_len[0, k]
            own = lax.div(table[adapters[g, req_slot[0, k]]], 8)
            owner_v[...] = jnp.where((row >= start) & (row < end), own, owner_v[...])
            return end

        lax.fori_loop(0, 16, mark, jnp.int32(0))

    pl.semaphore_wait(barrier, 13)

    class Gather:
        def __init__(self, name, lot, buf, own):
            self.name, self.lot, self.buf, self.own = name, lot, buf, own

        def block(self, half, i, j):
            return ys[j] * 4 + xs[i] if half == 0 else ys[i] * 4 + xs[j]

        def devs(self, half):
            return (dev_x, dev_y) if half == 0 else (dev_y, dev_x)

        def rows(self, half, i, j, quarter=None):
            b = self.block(half, i, j)
            start, size = (half * 192, 192) if quarter is None else (half * 192 + quarter * 96, 96)
            if len(self.buf.shape) == 3:
                return self.buf.at[b, pl.ds(start, size)]
            return self.buf.at[pl.ds(start, size), pl.ds(pl.multiple_of(b * 512, 512), 512)]

        def src_own(self, half):
            return self.own.at[pl.ds(half * 192, 192)]

        def key(self, *what):
            return (self.name,) + what

        def first_own(self, half):
            dev = self.devs(half)[0]
            for to in (2, 1):
                send(self.key(half, "own"), self.lot, self.src_own(half), self.rows(half, 0, 0), dev[to])

        def first_fwd(self, half):
            dev = self.devs(half)[0]
            got(self.key(half, "own"))
            for way in (0, 1):
                ref = self.rows(half, 1 + way, 0, way)
                send(self.key(half, "opp"), self.lot, ref, ref, dev[2 - way])

        def first_opp(self, half):
            got(self.key(half, "opp"))

        def second_own(self, half, i):
            dev = self.devs(half)[1]
            src = self.src_own(half) if i == 0 else self.rows(half, i, 0)
            for to in (2, 1):
                send(self.key(half, i), self.lot, src, self.rows(half, i, 0), dev[to])

        def second_fwd(self, half, i):
            dev = self.devs(half)[1]
            got(self.key(half, i))
            for way in (0, 1):
                ref = self.rows(half, i, 1 + way, way)
                send(self.key("last"), self.lot, ref, ref, dev[2 - way])

        def last(self):
            got(self.key("last"))

    hid = Gather("hid", 2, hid_all, hidden)
    out = Gather("out", 3, a_out, o_blk)

    def wrows(i, ch, grp, half=None):
        if half is None:
            return w_o.at[ys[i], pl.ds(2 * ch, 2), pl.ds(pl.multiple_of(grp * 64, 64), 64)]
        return w_o.at[ys[i], pl.ds(2 * ch, 2), pl.ds(pl.multiple_of(grp * 64 + half * 32, 32), 32)]

    def wrow(i, j, grp):
        return w_o.at[ys[i], j, pl.ds(pl.multiple_of(grp * 64, 64), 64)]

    def w_first(ch):
        for j in (2 * ch, 2 * ch + 1):
            for way, to in ((0, 2), (1, 1)):
                rows = pl.ds(pl.multiple_of(g * 64, 64), 64)
                send(("nbr", ch, way), 0, o_weight.at[rows, wcols(to, j)], wrow(0, j, g), dev_y[to])
                rows = pl.ds(pl.multiple_of(g * 64 + way * 32, 32), 32)
                send(("opp", ch), 0, o_weight.at[rows, wcols(3, j)], w_stage.at[way, j], dev_y[to])

    def w_second(ch):
        got(("opp", ch))
        for way in (0, 1):
            send(("opp2", ch), 0, w_stage.at[way, pl.ds(2 * ch, 2)], wrows(1 + way, ch, g, way), dev_y[2 - way])

    def w_spread(ch, i):
        got(("nbr", ch, i) if i < 2 else ("opp2", ch))
        ref = wrows(i + 1, ch, g)
        send(("z", ch, i), 0, ref, ref, dev_z[2])
        send(("z", ch, i), 0, ref, ref, dev_z[1])
        send(("sib", ch), 0, ref, ref, dev_sib)

    def w_pass(ch, i):
        got(("z", ch, i))
        for way in (0, 1):
            ref = wrows(i + 1, ch, gs[1 + way], way)
            send(("zopp", ch), 0, ref, ref, dev_z[2 - way])
        for way in (0, 1):
            ref = wrows(i + 1, ch, gs[1 + way])
            send(("sib", ch), 0, ref, ref, dev_sib)

    def w_last(ch):
        got(("zopp", ch))
        for i in range(3):
            ref = wrows(i + 1, ch, gs[3])
            send(("sib", ch), 0, ref, ref, dev_sib)

    def w_done(ch):
        got(("sib", ch))

    def adapters_send(name, first):
        for d in (4, 2, 6, 1, 3, 5, 7):
            rows = pl.ds(first, 128)
            send(name, 1, send_a.at[d, rows], recv_a.at[g, rows], {"group": mod(g + d, 8)})

    upper, lower = pl.ds(0, 192), pl.ds(192, 192)

    def attn_own():
        for to in (2, 1):
            send("attn", 2, attn, attn_all.at[y], dev_y[to])

    def attn_fwd():
        got("attn")
        for way, part_rows in ((0, upper), (1, lower)):
            ref = attn_all.at[ys[1 + way], part_rows]
            send("attn_opp", 2, ref, ref, dev_y[2 - way])

    def partial(j):
        def half(h, carry):
            rows = pl.ds(pl.multiple_of(h * 192, 192), 192)
            total = jnp.dot(attn_all[0, rows, :], w_o[0, j], preferred_element_type=F32)
            for i in range(1, 4):
                total = total + jnp.dot(attn_all[i, rows, :], w_o[i, j], preferred_element_type=F32)
            part[j, rows, :] = total
            return carry

        lax.fori_loop(0, 2, half, 0)

    lane = lax.broadcasted_iota(jnp.int32, (384, 128), 1)
    y_off = [mod(y + d, 4) for d in range(4)]

    def piece(v):
        return pl.ds(pl.multiple_of(v * 96, 32), 96)

    def down_product():
        down_v[...] = jnp.zeros((384, 128), F32)

        def down(o, carry):
            a = recv_a[o, 0:128, :]
            from_hid = lax.dot_general(hid_all[t], a, (((1,), (1,)), ((), ())), preferred_element_type=F32)
            from_att = lax.dot_general(attn_all[y], a, (((1,), (1,)), ((), ())), preferred_element_type=F32)
            value = jnp.where(lane < 64, from_hid, from_att)
            down_v[...] = jnp.where(owner_v[...] == o, value, down_v[...])
            return carry

        lax.fori_loop(0, 8, down, 0)
        for d in (1, 2, 3):
            send("down1", 1, down_v.at[piece(y_off[d])], down_1.at[d - 1], {"tensor": y_off[d] * 4 + x})

    def down_across():
        got("down1")
        down_s[0] = down_v[piece(y), :] + down_1[0] + down_1[1] + down_1[2]
        for d in (1, 2, 3):
            send("down2", 1, down_s.at[0], down_2.at[d - 1], {"tensor": y * 4 + mod(x + d, 4)})

    def down_back():
        got("down2")
        down_s[1] = down_s[0] + down_2[0] + down_2[1] + down_2[2]
        for d in (1, 2, 3):
            send("down3", 1, down_s.at[1], down_all.at[piece(y)], {"tensor": y_off[d] * 4 + x})
        down_all[piece(y), :] = down_s[1]

    def up_product():
        up_q[...] = jnp.zeros((384, 512), F32)
        up_o[...] = jnp.zeros((384, 512), F32)

        def up(o, carry):
            b = recv_a[o, 128:256, :]
            rows = jnp.where(owner_v[...] == o, down_all[...] * 0.5, 0.0)
            for keep, total in ((lane < 64, up_q), (lane >= 64, up_o)):
                kept = jnp.where(keep, rows, 0.0)
                high = kept.astype(BF16)
                low = (kept - high.astype(F32)).astype(BF16)
                total[...] += jnp.dot(high, b, preferred_element_type=F32) + jnp.dot(low, b, preferred_element_type=F32)
            return carry

        lax.fori_loop(0, 8, up, 0)

    def query_part(first, last):
        def query(k, carry):
            rows = pl.ds(pl.multiple_of(k * 512, 512), 512)
            up_q[...] += jnp.dot(hid_all[k], w_q[rows, :], preferred_element_type=F32)
            return carry

        lax.fori_loop(first, last, query, 0)

    w_first(0)
    hid.first_own(0)
    hid.first_own(1)
    hid.second_own(1, 0)
    pack_adapters()
    adapters_send("adp_a", 0)
    l_wq = load(4, q_weight, w_q)
    mark_rows()
    w_spread(0, 0)
    w_spread(0, 1)
    w_second(0)
    attn_own()
    hid.first_fwd(0)
    hid.first_fwd(1)
    hid.second_own(1, 1)
    hid.second_own(1, 2)
    w_spread(0, 2)
    w_first(1)
    loaded(1, l_hid)
    loaded(2, l_attn)
    got("adp_a")
    down_product()
    hid.second_fwd(1, 0)
    w_pass(0, 0)
    w_pass(0, 1)
    attn_fwd()
    w_pass(0, 2)
    w_spread(1, 0)
    w_spread(1, 1)
    w_second(1)
    hid.first_opp(1)
    hid.second_own(1, 3)
    hid.second_fwd(1, 1)
    hid.second_fwd(1, 2)
    w_last(0)
    loaded(3, l_wo)
    w_spread(1, 2)
    w_pass(1, 0)
    w_pass(1, 1)
    hid.second_fwd(1, 3)
    down_across()
    hid.second_own(0, 0)
    hid.second_own(0, 1)
    w_done(0)
    got("attn_opp")
    partial(0)
    send("red0", 1, part.at[0, upper], r_opp.at[0], dev_x[2])
    send("red1", 1, part.at[0, lower], r_opp.at[1], dev_x[1])
    partial(1)
    w_pass(1, 2)
    hid.second_own(0, 2)
    hid.first_opp(0)
    hid.second_own(0, 3)
    w_last(1)
    adapters_send("adp_b", 128)
    down_back()
    w_done(1)
    partial(2)
    send("red2", 1, part.at[1, lower], r_nbr.at[0, lower], dev_x[2])
    send("red3", 1, part.at[2, upper], r_nbr.at[1, upper], dev_x[1])
    hid.second_fwd(0, 0)
    hid.second_fwd(0, 1)
    got("red0")
    part[1, upper, :] = part[1, upper, :] + r_opp[0]
    send("red4", 1, part.at[1, upper], r_nbr.at[0, upper], dev_x[2])
    got("red1")
    part[2, lower, :] = part[2, lower, :] + r_opp[1]
    send("red5", 1, part.at[2, lower], r_nbr.at[1, lower], dev_x[1])
    partial(3)
    hid.second_fwd(0, 2)
    hid.second_fwd(0, 3)
    got("down3")
    got("adp_b")
    up_product()
    part[3] = part[3] + up_o[...]

    for k in (2, 3, 4, 5):
        got(f"red{k}")
    own_cols = pl.ds(pl.multiple_of(t * 512, 512), 512)
    o_blk[...] = (part[3] + r_nbr[0] + r_nbr[1]).astype(BF16)
    out.first_own(0)
    out.first_own(1)
    l_o = load(5, o_blk, a_out.at[:, own_cols])
    hid.last()
    loaded(4, l_wq)
    query_part(0, 8)
    out.second_own(1, 0)
    out.second_own(0, 0)
    for lot in (0, 1, 2):
        gone(lot)
    out.first_fwd(0)
    out.first_fwd(1)
    for i in (1, 2):
        out.second_own(0, i)
        out.second_own(1, i)
    query_part(8, 12)
    out.first_opp(0)
    out.second_own(0, 3)
    out.first_opp(1)
    out.second_own(1, 3)
    out.second_fwd(0, 0)
    out.second_fwd(1, 0)
    out.second_fwd(0, 1)
    out.second_fwd(1, 1)
    query_part(12, 16)
    q_blk[...] = up_q[...].astype(BF16)
    l_q = load(6, q_blk, q_out)
    for i in (2, 3):
        out.second_fwd(0, i)
        out.second_fwd(1, i)
    out.last()
    gone(3)
    loaded(5, l_o)
    loaded(6, l_q)


def body(hidden, attn, q_weight, o_weight, table, adapters, req_slot, req_len, qa, qb, oa, ob):
    hbm = pl.BlockSpec(memory_space=pl.ANY)
    smem = pl.BlockSpec(memory_space=pltpu.SMEM)
    vm = pltpu.VMEM
    qa_t, oa_t = jnp.transpose(qa, (0, 2, 1)), jnp.transpose(oa, (0, 2, 1))
    return pl.pallas_call(
        kernel,
        out_shape=(
            vm((384, 512), BF16),
            vm((384, 8192), BF16),
        ),
        in_specs=[hbm] * 8 + [smem] * 4,
        out_specs=[hbm] * 2,
        scratch_shapes=[
            vm((16, 384, 512), BF16),
            vm((4, 384, 512), BF16),
            vm((4, 4, 512, 512), BF16),
            vm((2, 4, 32, 512), BF16),
            vm((8192, 512), BF16),
            vm((8, 64, 512), BF16),
            vm((8, 64, 512), BF16),
            vm((8, 64, 512), BF16),
            vm((8, 64, 512), BF16),
            vm((8, 256, 512), BF16),
            vm((8, 256, 512), BF16),
            vm((384, 128), jnp.int32),
            vm((384, 128), F32),
            vm((3, 96, 128), F32),
            vm((3, 96, 128), F32),
            vm((2, 96, 128), F32),
            vm((384, 128), F32),
            vm((384, 512), F32),
            vm((384, 512), F32),
            vm((4, 384, 512), F32),
            vm((2, 192, 512), F32),
            vm((2, 384, 512), F32),
            vm((384, 512), BF16),
            vm((384, 512), BF16),
            pltpu.SemaphoreType.DMA((N_SEND,)),
            pltpu.SemaphoreType.DMA((N_RECV,)),
            pltpu.SemaphoreType.DMA((N_LOCAL,)),
        ],
        compiler_params=pltpu.CompilerParams(
            collective_id=0, has_side_effects=True, vmem_limit_bytes=48 * 1024 * 1024
        ),
    )(hidden, attn, q_weight, o_weight, qa_t, qb, oa_t, ob, table, adapters, req_slot, req_len)


def solution(mesh):
    return jax.shard_map(
        body,
        mesh=mesh,
        in_specs=(
            P("group", "tensor"),
            P("group", "tensor"),
            P(None, "tensor"),
            P("tensor", None),
            P(),
            P(),
            P("group", None),
            P("group", None),
            P("group", "tensor", None),
            P("group", None, "tensor"),
            P("group", "tensor", None),
            P("group", None, "tensor"),
        ),
        out_specs=(P("group", "tensor"), P("group", None)),
        check_vma=False,
    )
```

time: 466 us -> 113 us (0.24)
  blocking collectives: 290 us -> 0 us
  Pallas kernels: 0 us -> 109 us
  waiting for transfers between devices: 108 us -> 0 us
  matrix products: 23 us -> 0 us
  starting transfers between devices: 15.6 us -> 0 us
  between operations: 14.3 us -> 0.64 us
  other arithmetic: 6.07 us -> 0 us
  local copies, waits for them, and re-layouts: 8.43 us -> 3.45 us
    psum x1 -> x0, blocking collectives: 277 us -> none  [body(): attn_out = lax.psum(o_term, 'tensor').astype(jnp.bfloat16)]
    pallas_call x0 -> x1, Pallas kernels: none -> 109 us  [body(): pl.pallas_call(kernel, out_shape=(vm((384, 512), BF16), vm((384, 8192), B...]
    psum x1 -> x0, waiting for transfers between devices: 50 us -> none  [body(): q_down, o_down = lax.psum((q_partial, output_partial_sum), 'tensor')]
    all_gather x1 -> x0, waiting for transfers between devices: 39.2 us -> none  [body(): lax.all_gather(hidden_rows, 'tensor', axis=1, tiled=True)]
    dot_general x6 -> x0, matrix products: 23 us -> none  [the longest x1 9.77 us: body(): o_term = jnp.dot(attn_rows, o_weight, preferred_element_type=jnp.float32)]
    all_to_all x3 -> x0, waiting for transfers between devices: 17.8 us -> none  [the longest x1 9.1 us: body(): lax.all_to_all(pack(qa_store), 'group', split_axis=0, concat_axis=0, tile...]
    all_to_all x3 -> x0, starting transfers between devices: 15.6 us -> none  [the longest x1 6.8 us: body(): lax.all_to_all(pack(qa_store), 'group', split_axis=0, concat_axis=0, tile...]
    all_to_all x1 -> x0, blocking collectives: 12.7 us -> none  [body(): lax.all_to_all(pack(ob_store), 'group', split_axis=0, concat_axis=0, tile...]
  transfers between devices with their start and end apart: 5 -> 0, of which waited for: 4 -> 0; matrix products, arithmetic and copies ran while one was open for 4% -> 0% of each run, Pallas kernels for 0% -> 0%
where the time goes in v3:
time: 113 us
  Pallas kernels  109 us (96%)
  local copies, waits for them, and re-layouts  3.45 us (3%)
    pallas_call x1, Pallas kernels, body(): pl.pallas_call(kernel, out_shape=(vm((384, 512), BF16), vm((384, 8192), B...  109 us
    unnamed x2, local copies, waits for them, and re-layouts  3.45 us

profile of v3, /device:TPU:1, one launch (start us, length us, event | category | flops | bytes accessed | tf_op | source)
XLA Modules:
  0.0 113.1 jit_solution(17880288329440946552)
XLA Ops:
  0.6 109.0 %shard_map.131 = (bf16[384,512]{1,0:T(8,128)(2,1)S(1)}, bf16[384,8192]{1,0:T(8,128)(2,1)S(1)}) custom-call(bf16[384,512]{1,0:T(8,128)(2,1)} %hidden.1, bf16[384,512]{1,0:T(8,128)(2,1)} %attn.1, bf16[8192,512]{1,0:T(8,128)(2,1)} %q_weight.1, bf16[512,8192]{1,0:T(8,128)(2,1)} %o_weight.1, bf16[8,64,512]{2,1,0:T(8,128)(2,1)} %bitcast.2, ...), custom_call_target="tpu_custom_call" | custom-call | tf_op jit(solution)/shard_map/pallas_call | solution.py:436
  109.7 0.7 copy.16
  110.4 2.7 %copy.17 = bf16[384,8192]{1,0:T(8,128)(2,1)} copy(bf16[384,8192]{1,0:T(8,128)(2,1)S(1)} %get-tuple-element.3) | data formatting | bytes 12582912
